TPU v7x, 512 devices: a whole 4x8x8 slice. The times are simulated.
512 devices in a mesh: cell: 32 (over y_hi, z, core), gene: 16 (over y_lo, x).
Axes of the slice: x: 4, y: 8 (y_hi: 2, y_lo: 4; y = y_hi * 4 + y_lo), z: 8, core: 2. Of those that a mesh axis runs over, the one named last changes fastest.
Arguments:
- counts: int32 [8192, 16384], P('cell', 'gene'), may hold values from 0 to 54, as said below
- cell_totals: int32 [8192], P('cell'), may hold values from 32768 to 294912, as said below
- gene_totals: int32 [16384], P('gene'), may hold values from 997 to 2991, as said below
- test_matrix: bfloat16 [16384, 96], P('gene', 'cell'), may hold values from -0.046875 to 0.046875
Outputs:
- sketch: bfloat16 [8192, 96], P('cell')
- gene_panel: bfloat16 [16384, 96], P('gene')
Inputs may be any that keep to these rules, and one draw needn't show every extreme that they name: counts are nonnegative. `cell_totals`: cell totals are positive. `gene_totals`: gene totals are positive.
All inputs are finite; a program needn't handle non-finite values.
Results may differ from a plain program's by a relative error of at most 0.03.
Values may be sent and summed in bfloat16 or wider, within the bound.
No kernel may reach another device: no remote copies, remote signals or barrier semaphores. Data moves between devices by JAX's collectives and lax.ppermute only.
A program may use at most 64 MiB of HBM per device.

v0:
```python
import math
import jax
import jax.numpy as jnp
from jax import lax
from jax.sharding import PartitionSpec as P

ITERS = 3


def pearson(counts, cell_totals, fraction):
    expected = cell_totals.astype(jnp.float32)[:, None] * fraction[None, :]
    spread = jnp.sqrt(expected + expected * expected / 100.0)
    return ((counts.astype(jnp.float32) - expected) / spread).astype(jnp.bfloat16)


def transposed_product(left, right):
    return lax.dot_general(
        left, right, (((0,), (0,)), ((), ())), preferred_element_type=jnp.float32
    )


def shards(counts, cell_totals, gene_totals, test_matrix):
    cell_rows = counts.shape[0]
    gene_cols = counts.shape[1]
    scale = 1.0 / math.sqrt(cell_rows * lax.axis_size("cell") + gene_cols * lax.axis_size("gene"))
    total = lax.psum(jnp.sum(gene_totals), "gene")
    fraction = gene_totals.astype(jnp.float32) / total.astype(jnp.float32)
    stored = pearson(counts, cell_totals, fraction)

    def cell_side(panel, factor):
        partial_sum = jnp.dot(stored, panel, preferred_element_type=jnp.float32)
        return (
            lax.psum(partial_sum.astype(jnp.bfloat16), "gene").astype(jnp.float32) * factor
        ).astype(jnp.bfloat16)

    def gene_side(sketch):
        partial_sum = transposed_product(stored, sketch)
        return (
            lax.psum(partial_sum.astype(jnp.bfloat16), "cell").astype(jnp.float32) * scale
        ).astype(jnp.bfloat16)

    test_block = lax.all_gather(test_matrix, "cell", axis=1, tiled=True)
    sketch = cell_side(test_block, 1.0)
    for step in range(ITERS):
        panel = gene_side(sketch)
        sketch = cell_side(panel, scale)
    gene_panel = gene_side(sketch)
    return (sketch, gene_panel)


def solution(mesh):
    in_specs = (P("cell", "gene"), P("cell"), P("gene"), P("gene", "cell"))
    out_specs = (P("cell", None), P("gene", None))
    return jax.shard_map(shards, mesh=mesh, in_specs=in_specs, out_specs=out_specs, check_vma=False)
```

profile of v0, /device:TPU:1, one launch (start us, length us, event | category | flops | bytes accessed | tf_op | source)
XLA Modules:
  0.0 1696.3 jit_solution(1794556545460910786)
XLA Ops:
  7.2 0.0 all-reduce.5.cloned.1.call-start
  7.2 0.0 copy-start.3
  7.2 1.3 reduce_sum.9
  8.5 0.0 copy-start.1
  8.6 0.0 copy-start.2
  8.6 13.9 psum.63
  23.1 0.0 copy-done.3
  23.2 0.0 copy-done.1
  23.2 0.0 copy-done.2
  23.2 62.6 %all-gather = bf16[32,3,1024]{2,1,0:T(4,128)(2,1)S(1)} all-gather(bf16[1,3,1024]{2,1,0:T(4,128)(2,1)S(1)} %bitcast.14), channel_id=1, replica_groups=mesh['cell'=32,'gene'=16] {'cell'}, dimensions={0}, use_global_device_ids=true | all-gather | bytes 202752 | tf_op jit(solution)/shard_map/all_gather | solution.py:42
  85.8 0.2 reshape.7
  85.9 1.6 fusion.1
  87.5 0.3 convolution_convert_fusion.7
  87.8 63.7 %psum.64 = bf16[256,96]{0,1:T(8,128)(2,1)S(1)} all-reduce(bf16[256,96]{0,1:T(8,128)(2,1)S(1)} %convolution_convert_fusion.7), channel_id=1, replica_groups=mesh['cell'=32,'gene'=16] {'gene'}, use_global_device_ids=true, to_apply=%region_2.0 | all-reduce | flops 24576 | bytes 98304 | tf_op jit(solution)/shard_map/psum | solution.py:33
  151.5 0.9 convolution_convert_fusion.3
  152.4 0.0 all-reduce.5.cloned.1.call-update
  152.4 0.0 all-reduce.7.cloned.1.call-start
  152.5 330.0 %all-reduce.5.cloned.1.call-done = bf16[1024,96]{0,1:T(8,128)(2,1)} async-done(((bf16[1024,96]{0,1:T(8,128)(2,1)}), bf16[1024,96]{0,1:T(8,128)(2,1)}) %all-reduce.5.cloned.1.call-update) | async-done | bytes 196624 | tf_op jit(solution)/shard_map/psum | solution.py:39
  482.5 1.2 convolution_convert_fusion.6
  483.8 63.0 %psum.66 = bf16[256,96]{0,1:T(8,128)(2,1)S(1)} all-reduce(bf16[256,96]{0,1:T(8,128)(2,1)S(1)} %convolution_convert_fusion.6), channel_id=1, replica_groups=mesh['cell'=32,'gene'=16] {'gene'}, use_global_device_ids=true, to_apply=%region_4.0 | all-reduce | flops 24576 | bytes 98304 | tf_op jit(solution)/shard_map/psum | solution.py:33
  546.8 0.9 convolution_convert_fusion.2
  547.7 0.0 all-reduce.7.cloned.1.call-update
  547.7 0.0 all-reduce.9.cloned.1.call-start
  547.8 336.6 %all-reduce.7.cloned.1.call-done = bf16[1024,96]{0,1:T(8,128)(2,1)} async-done(((bf16[1024,96]{0,1:T(8,128)(2,1)}), bf16[1024,96]{0,1:T(8,128)(2,1)}) %all-reduce.7.cloned.1.call-update) | async-done | bytes 196624 | tf_op jit(solution)/shard_map/psum | solution.py:39
  884.4 1.2 convolution_convert_fusion.5
  885.6 63.0 %psum.68 = bf16[256,96]{0,1:T(8,128)(2,1)S(1)} all-reduce(bf16[256,96]{0,1:T(8,128)(2,1)S(1)} %convolution_convert_fusion.5), channel_id=1, replica_groups=mesh['cell'=32,'gene'=16] {'gene'}, use_global_device_ids=true, to_apply=%region_6.0 | all-reduce | flops 24576 | bytes 98304 | tf_op jit(solution)/shard_map/psum | solution.py:33
  948.6 0.9 convolution_convert_fusion.1
  949.6 0.0 all-reduce.9.cloned.1.call-update
  949.6 0.0 all-reduce.11.cloned.1.call-start
  949.6 336.6 %all-reduce.9.cloned.1.call-done = bf16[1024,96]{0,1:T(8,128)(2,1)} async-done(((bf16[1024,96]{0,1:T(8,128)(2,1)}), bf16[1024,96]{0,1:T(8,128)(2,1)}) %all-reduce.9.cloned.1.call-update) | async-done | bytes 196624 | tf_op jit(solution)/shard_map/psum | solution.py:39
  1286.2 1.2 convolution_convert_fusion.4
  1287.5 63.0 %psum.70 = bf16[256,96]{0,1:T(8,128)(2,1)S(1)} all-reduce(bf16[256,96]{0,1:T(8,128)(2,1)S(1)} %convolution_convert_fusion.4), channel_id=1, replica_groups=mesh['cell'=32,'gene'=16] {'gene'}, use_global_device_ids=true, to_apply=%region_8.0 | all-reduce | flops 24576 | bytes 98304 | tf_op jit(solution)/shard_map/psum | solution.py:33
  1350.5 0.0 copy-start
  1350.5 0.9 convolution_convert_fusion
  1351.4 0.0 copy-done
  1351.4 0.0 all-reduce.11.cloned.1.call-update
  1351.4 336.7 %all-reduce.11.cloned.1.call-done = bf16[1024,96]{0,1:T(8,128)(2,1)} async-done(((bf16[1024,96]{0,1:T(8,128)(2,1)}), bf16[1024,96]{0,1:T(8,128)(2,1)}) %all-reduce.11.cloned.1.call-update) | async-done | bytes 196624 | tf_op jit(solution)/shard_map/psum | solution.py:39
  1688.1 1.6 multiply_convert_fusion
  (3 shorter events, 0.0 us)
Async XLA Ops:
  7.2 475.4 %all-reduce.5.cloned.1.call-start = ((), (), s32[]{:S(2)}) async-start(), calls=%async_computation | async-start | bytes 393216 | tf_op jit(solution)/shard_map/psum | solution.py:39
  7.2 15.9 copy-start.3
  8.5 14.6 copy-start.1
  8.6 14.6 copy-start.2
  152.4 731.9 %all-reduce.7.cloned.1.call-start = ((), (), s32[]{:S(2)}) async-start(), calls=%async_computation.1 | async-start | bytes 393216 | tf_op jit(solution)/shard_map/psum | solution.py:39
  547.7 738.5 %all-reduce.9.cloned.1.call-start = ((), (), s32[]{:S(2)}) async-start(), calls=%async_computation.2 | async-start | bytes 393216 | tf_op jit(solution)/shard_map/psum | solution.py:39
  949.6 738.5 %all-reduce.11.cloned.1.call-start = ((), (), s32[]{:S(2)}) async-start(), calls=%async_computation.3 | async-start | bytes 393216 | tf_op jit(solution)/shard_map/psum | solution.py:39
  1350.5 0.9 copy-start
Sparse Core Ops, SparseCore 0:
  152.6 329.9 all-reduce.4
  547.8 336.4 all-reduce.6
  949.7 336.4 all-reduce.8
  1351.6 336.4 all-reduce.10
where the time goes:
time: 1700 us
  waiting for transfers between devices  1340 us (79%)
  blocking collectives  329 us (19%)
    psum x4, waiting for transfers between devices, gene_side(): lax.psum(partial_sum.astype(jnp.bfloat16), 'cell').astype(jnp.float32)  1340 us
    psum x4, blocking collectives, cell_side(): lax.psum(partial_sum.astype(jnp.bfloat16), 'gene').astype(jnp.float32)  253 us
    all_gather x1, blocking collectives, shards(): test_block = lax.all_gather(test_matrix, 'cell', axis=1, tiled=True)  62.6 us
  transfers between devices with their start and end apart: 4, of which 4 were waited for; matrix products, arithmetic and copies ran while one was open for 0% of the time, Pallas kernels for 0%

commit v1 on v0

--- a/solution.py
+++ b/solution.py
@@ -30,7 +30,10 @@
     def cell_side(panel, factor):
         partial_sum = jnp.dot(stored, panel, preferred_element_type=jnp.float32)
         return (
-            lax.psum(partial_sum.astype(jnp.bfloat16), "gene").astype(jnp.float32) * factor
+            jnp.sum(lax.all_gather(partial_sum.astype(jnp.bfloat16), "gene"), axis=0).astype(
+                jnp.float32
+            )
+            * factor
         ).astype(jnp.bfloat16)
 
     def gene_side(sketch):

time: 1700 us -> 1570 us (0.924)
  blocking collectives: 329 us -> 227 us
  waiting for transfers between devices: 1340 us -> 1310 us
    psum x4 -> x0, blocking collectives: 253 us -> none  [cell_side(): lax.psum(partial_sum.astype(jnp.bfloat16), 'gene').astype(jnp.float32)]
    all_gather x0 -> x4, blocking collectives: none -> 150 us  [cell_side(): lax.all_gather(partial_sum.astype(jnp.bfloat16), 'gene')]
    psum x4, waiting for transfers between devices: 1340 us -> 1310 us  [gene_side(): lax.psum(partial_sum.astype(jnp.bfloat16), 'cell').astype(jnp.float32)]
where the time goes in v1:
time: 1570 us
  waiting for transfers between devices  1310 us (83%)
  blocking collectives  227 us (14%)
    psum x4, waiting for transfers between devices, gene_side(): lax.psum(partial_sum.astype(jnp.bfloat16), 'cell').astype(jnp.float32)  1310 us
    all_gather x4, blocking collectives, cell_side(): lax.all_gather(partial_sum.astype(jnp.bfloat16), 'gene')  150 us
    all_gather x1, blocking collectives, shards(): test_block = lax.all_gather(test_matrix, 'cell', axis=1, tiled=True)  62.6 us
  transfers between devices with their start and end apart: 4, of which 4 were waited for; matrix products, arithmetic and copies ran while one was open for 0% of the time, Pallas kernels for 0%

profile of v1, /device:TPU:1, one launch (start us, length us, event | category | flops | bytes accessed | tf_op | source)
XLA Modules:
  0.0 1566.1 jit_solution(16032575909564136851)
XLA Ops:
  7.2 0.0 all-reduce.5.cloned.1.call-start
  7.2 0.0 copy-start.3
  7.2 1.3 reduce_sum.57
  8.5 0.0 copy-start.1
  8.6 0.0 copy-start.2
  8.6 13.9 psum.35
  23.1 0.0 copy-done.3
  23.2 0.0 copy-done.1
  23.2 0.0 copy-done.2
  23.2 62.6 %all-gather.4 = bf16[32,3,1024]{2,1,0:T(4,128)(2,1)S(1)} all-gather(bf16[1,3,1024]{2,1,0:T(4,128)(2,1)S(1)} %bitcast.38), channel_id=1, replica_groups=mesh['cell'=32,'gene'=16] {'cell'}, dimensions={0}, use_global_device_ids=true | all-gather | bytes 202752 | tf_op jit(solution)/shard_map/all_gather | solution.py:45
  85.8 0.2 reshape.11
  85.9 1.6 fusion.1
  87.5 0.3 convolution_convert_fusion.7
  87.8 37.7 %all-gather = bf16[4096,96]{0,1:T(8,128)(2,1)S(1)} all-gather(bf16[256,96]{0,1:T(8,128)(2,1)S(1)} %convolution_convert_fusion.7), channel_id=2, replica_groups=mesh['cell'=32,'gene'=16] {'gene'}, dimensions={0}, use_global_device_ids=true | all-gather | bytes 835584 | tf_op jit(solution)/shard_map/all_gather | solution.py:33
  125.5 0.2 copy.6
  125.7 0.4 bitcast_reduce_fusion.3
  126.1 0.9 convolution_convert_fusion.3
  127.0 0.0 all-reduce.5.cloned.1.call-update
  127.0 0.0 all-reduce.7.cloned.1.call-start
  127.0 323.6 %all-reduce.5.cloned.1.call-done = bf16[1024,96]{0,1:T(8,128)(2,1)} async-done(((bf16[1024,96]{0,1:T(8,128)(2,1)}), bf16[1024,96]{0,1:T(8,128)(2,1)}) %all-reduce.5.cloned.1.call-update) | async-done | bytes 196624 | tf_op jit(solution)/shard_map/psum | solution.py:42
  450.6 1.2 convolution_convert_fusion.6
  451.8 37.4 %all-gather.1 = bf16[4096,96]{0,1:T(8,128)(2,1)S(1)} all-gather(bf16[256,96]{0,1:T(8,128)(2,1)S(1)} %convolution_convert_fusion.6), channel_id=3, replica_groups=mesh['cell'=32,'gene'=16] {'gene'}, dimensions={0}, use_global_device_ids=true | all-gather | bytes 835584 | tf_op jit(solution)/shard_map/all_gather | solution.py:33
  489.3 0.2 copy.7
  489.4 0.4 bitcast_reduce_fusion.2
  489.8 0.9 convolution_convert_fusion.2
  490.7 0.0 all-reduce.7.cloned.1.call-update
  490.7 0.0 all-reduce.9.cloned.1.call-start
  490.8 328.9 %all-reduce.7.cloned.1.call-done = bf16[1024,96]{0,1:T(8,128)(2,1)} async-done(((bf16[1024,96]{0,1:T(8,128)(2,1)}), bf16[1024,96]{0,1:T(8,128)(2,1)}) %all-reduce.7.cloned.1.call-update) | async-done | bytes 196624 | tf_op jit(solution)/shard_map/psum | solution.py:42
  819.7 1.2 convolution_convert_fusion.5
  820.9 37.4 %all-gather.2 = bf16[4096,96]{0,1:T(8,128)(2,1)S(1)} all-gather(bf16[256,96]{0,1:T(8,128)(2,1)S(1)} %convolution_convert_fusion.5), channel_id=4, replica_groups=mesh['cell'=32,'gene'=16] {'gene'}, dimensions={0}, use_global_device_ids=true | all-gather | bytes 835584 | tf_op jit(solution)/shard_map/all_gather | solution.py:33
  858.4 0.2 copy.8
  858.5 0.4 bitcast_reduce_fusion.1
  858.9 0.9 convolution_convert_fusion.1
  859.8 0.0 all-reduce.9.cloned.1.call-update
  859.8 0.0 all-reduce.11.cloned.1.call-start
  859.9 328.9 %all-reduce.9.cloned.1.call-done = bf16[1024,96]{0,1:T(8,128)(2,1)} async-done(((bf16[1024,96]{0,1:T(8,128)(2,1)}), bf16[1024,96]{0,1:T(8,128)(2,1)}) %all-reduce.9.cloned.1.call-update) | async-done | bytes 196624 | tf_op jit(solution)/shard_map/psum | solution.py:42
  1188.8 1.2 convolution_convert_fusion.4
  1190.0 37.5 %all-gather.3 = bf16[4096,96]{0,1:T(8,128)(2,1)S(1)} all-gather(bf16[256,96]{0,1:T(8,128)(2,1)S(1)} %convolution_convert_fusion.4), channel_id=5, replica_groups=mesh['cell'=32,'gene'=16] {'gene'}, dimensions={0}, use_global_device_ids=true | all-gather | bytes 835584 | tf_op jit(solution)/shard_map/all_gather | solution.py:33
  1227.5 0.2 copy.9
  1227.6 0.4 bitcast_reduce_fusion
  1228.0 0.0 copy-start
  1228.0 0.9 convolution_convert_fusion
  1229.0 0.0 copy-done
  1229.0 0.0 all-reduce.11.cloned.1.call-update
  1229.0 328.9 %all-reduce.11.cloned.1.call-done = bf16[1024,96]{0,1:T(8,128)(2,1)} async-done(((bf16[1024,96]{0,1:T(8,128)(2,1)}), bf16[1024,96]{0,1:T(8,128)(2,1)}) %all-reduce.11.cloned.1.call-update) | async-done | bytes 196624 | tf_op jit(solution)/shard_map/psum | solution.py:42
  1557.9 1.6 multiply_convert_fusion
  (3 shorter events, 0.0 us)
Async XLA Ops:
  7.2 443.4 %all-reduce.5.cloned.1.call-start = ((), (), s32[]{:S(2)}) async-start(), calls=%async_computation | async-start | bytes 393216 | tf_op jit(solution)/shard_map/psum | solution.py:42
  7.2 15.9 %copy-start.3 = (s32[256]{0:T(256)S(1)}, s32[256]{0:T(256)}, u32[]{:S(2)}) copy-start(s32[256]{0:T(256)} %param.5) | copy-start | bytes 3076
  8.5 14.6 copy-start.1
  8.6 14.6 copy-start.2
  127.0 692.7 %all-reduce.7.cloned.1.call-start = ((), (), s32[]{:S(2)}) async-start(), calls=%async_computation.1 | async-start | bytes 393216 | tf_op jit(solution)/shard_map/psum | solution.py:42
  490.7 698.0 %all-reduce.9.cloned.1.call-start = ((), (), s32[]{:S(2)}) async-start(), calls=%async_computation.2 | async-start | bytes 393216 | tf_op jit(solution)/shard_map/psum | solution.py:42
  859.8 698.1 %all-reduce.11.cloned.1.call-start = ((), (), s32[]{:S(2)}) async-start(), calls=%async_computation.3 | async-start | bytes 393216 | tf_op jit(solution)/shard_map/psum | solution.py:42
  1228.0 0.9 copy-start
Sparse Core Ops, SparseCore 0:
  127.1 323.4 all-reduce.4
  490.9 328.7 all-reduce.6
  860.0 328.7 all-reduce.8
  1229.1 328.7 all-reduce.10
